TPU v7x, 128 devices: a whole 4x4x4 slice. The times are simulated.
128 devices in a mesh: seg: 16 (over z, y_lo, core), section: 8 (over y_hi, x).
Axes of the slice: x: 4, y: 4 (y_hi: 2, y_lo: 2; y = y_hi * 2 + y_lo), z: 4, core: 2. Of those that a mesh axis runs over, the one named last changes fastest.
Arguments:
- leaving: bfloat16 [16, 8, 272, 4096], P('seg', 'section'), may hold values from -6 to 6
- w_query: bfloat16 [8, 4096, 2048], P('section'), may hold values from -0.09375 to 0.09375
- w_key: bfloat16 [8, 4096, 2048], P('section', None, 'seg'), may hold values from -0.09375 to 0.09375
- w_value: bfloat16 [8, 4096, 4096], P('section', None, 'seg'), may hold values from -0.09375 to 0.09375
- w_gate: bfloat16 [8, 4096], P('section'), may hold values from -0.09375 to 0.09375
- norm_gain: bfloat16 [8, 4096], P('section'), may hold values from 0.5 to 1.5
- memory_matrix: bfloat16 [8, 4096, 2048], P('section', 'seg'), may hold values from -24 to 24
- key_totals: float32 [8, 2048], P('section'), may hold values from 0.02 to 0.5
- doc_starts: int32 [8, 16], P('section'), may hold values 0 or 1
Outputs:
- updated: bfloat16 [16, 8, 272, 4096], P('seg', 'section')
- matrix_next: bfloat16 [8, 4096, 2048], P('section', 'seg')
- totals_next: float32 [8, 2048], P('section')
All inputs are finite; a program needn't handle non-finite values. No bound on the sum of `doc_starts` on one device may be relied on, other than what follows from the above.
Results may differ from a plain program's by a relative error of at most 0.01.
Values may be sent and summed in bfloat16 or wider, within the bound.
No kernel may reach another device: no remote copies, remote signals or barrier semaphores. Data moves between devices by JAX's collectives and lax.ppermute only.
A program may use at most 128 MiB of HBM per device.

v0:
```python
import jax
import jax.numpy as jnp
from jax import lax
from jax.sharding import PartitionSpec as P

MEM = 16
highest = lax.Precision.HIGHEST
epsilon = 1e-05


def shifted(shard, axis, by):
    size = lax.axis_size(axis)
    return lax.ppermute(shard, axis, [(i, (i + by) % size) for i in range(size)])


def from_root(block, axis, source):
    block = jnp.where(lax.axis_index(axis) == source, block, jnp.zeros_like(block))
    return lax.psum(block, axis)


def feature_map(projected):
    return jax.nn.elu(projected) + 1.0


def contract_last(left_rows, right_rows):
    return lax.dot_general(
        left_rows, right_rows, (((1,), (1,)), ((), ())), preferred_element_type=jnp.float32
    )


def contract_first(left_rows, right_rows):
    return lax.dot_general(
        left_rows,
        right_rows,
        (((0,), (0,)), ((), ())),
        precision=highest,
        preferred_element_type=jnp.float32,
    )


def visibility(starts_row):
    seg_total = starts_row.shape[0]
    positions = jnp.arange(seg_total, dtype=jnp.int32)
    last_start = lax.cummax(jnp.where(starts_row == 1, positions, jnp.int32(-1)), axis=0)
    fresh_flag = (last_start < 0).astype(jnp.float32)
    seen_pairs = (
        (positions[:, None] >= last_start[None, :]) & (positions[:, None] < positions[None, :])
    ).astype(jnp.float32)
    seen_final = (positions >= last_start[seg_total - 1]).astype(jnp.float32)
    return (fresh_flag, seen_pairs, seen_final)


def local(
    leaving, w_query, w_key, w_value, w_gate, norm_gain, memory_matrix, key_totals, doc_starts
):
    entering = shifted(leaving, "section", 1)[0, 0]
    row_count = entering.shape[0]
    feature_count = entering.shape[1]
    seg_count = lax.axis_size("seg")
    my_index = lax.axis_index("seg")
    wide_rows = entering.astype(jnp.float32)
    inverse_rms = lax.rsqrt(jnp.mean(wide_rows * wide_rows, axis=-1, keepdims=True) + epsilon)
    normed = (wide_rows * inverse_rms * norm_gain[0].astype(jnp.float32)).astype(jnp.bfloat16)
    queries = feature_map(jnp.dot(normed, w_query[0], preferred_element_type=jnp.float32)).astype(
        jnp.bfloat16
    )
    memory = lax.all_gather(normed[:MEM], "seg", axis=0, tiled=True)
    key_part = feature_map(jnp.dot(memory, w_key[0], preferred_element_type=jnp.float32)).astype(
        jnp.bfloat16
    )
    value_part = jnp.dot(memory, w_value[0], preferred_element_type=jnp.float32)
    gate_rates = jax.nn.sigmoid(jnp.dot(memory, w_gate[0], preferred_element_type=jnp.float32))
    key_rows = lax.all_gather(key_part, "seg", axis=1, tiled=True)
    values = lax.all_to_all(
        value_part.reshape(seg_count, MEM, value_part.shape[1]).astype(jnp.bfloat16),
        "seg",
        split_axis=0,
        concat_axis=2,
        tiled=True,
    ).astype(jnp.float32)[0]
    fresh_flag, seen_pairs, seen_final = visibility(doc_starts[0])
    key_wide = key_rows.astype(jnp.float32)
    key_sums = key_wide.reshape(seg_count, MEM, -1).sum(axis=1)
    totals = fresh_flag[:, None] * key_totals[0][None, :] + jnp.dot(
        seen_pairs.T, key_sums, precision=highest
    )
    total_rows = jnp.repeat(totals, MEM, axis=0)
    key_scales = jnp.maximum(jnp.sum(total_rows * key_wide, axis=-1), 1.0)
    key_gram = contract_last(key_rows, key_rows)
    seen_cols = jnp.repeat(jnp.repeat(seen_pairs, MEM, axis=0), MEM, axis=1)
    mixing = seen_cols * key_gram * (gate_rates / key_scales)[None, :]
    my_keys = lax.dynamic_slice_in_dim(key_rows, my_index * MEM, MEM, 0)
    probes = jnp.concatenate([queries, my_keys], axis=0)
    probed_all = contract_last(probes, lax.all_gather(memory_matrix[0], "seg", axis=0, tiled=True))
    base_read = probed_all[:row_count]
    probed_keys = probed_all[row_count:]
    my_fresh = fresh_flag[my_index]
    my_rates = lax.dynamic_slice_in_dim(gate_rates, my_index * MEM, MEM, 0)
    my_scales = lax.dynamic_slice_in_dim(key_scales, my_index * MEM, MEM, 0)
    initial = my_rates[:, None] * (values - my_fresh * probed_keys / my_scales[:, None])
    writes = jnp.zeros((seg_count * MEM, feature_count), jnp.float32)

    def relay_step(step_index, current):
        mix_cols = lax.dynamic_slice_in_dim(mixing, step_index * MEM, MEM, 1)
        candidate = initial - contract_first(mix_cols, current)
        arrived = from_root(candidate.astype(jnp.bfloat16), "seg", step_index).astype(
            candidate.dtype
        )
        return lax.dynamic_update_slice_in_dim(current, arrived, step_index * MEM, 0)

    writes = lax.fori_loop(0, seg_count, relay_step, writes)
    column_mask = jnp.repeat(seen_pairs[:, my_index], MEM)
    similarity = contract_last(queries, key_rows) * column_mask[None, :]
    low_rank = jnp.dot(similarity, writes, precision=highest)
    my_totals = lax.dynamic_slice_in_dim(totals, my_index, 1, 0)
    denominator = jnp.maximum(jnp.sum(queries.astype(jnp.float32) * my_totals, axis=-1), 1.0)
    updated = (wide_rows + (my_fresh * base_read + low_rank) / denominator[:, None]).astype(
        jnp.bfloat16
    )
    slab_width = memory_matrix.shape[1]
    write_cols = lax.dynamic_slice_in_dim(writes, my_index * slab_width, slab_width, 1)
    end_rows = jnp.repeat(seen_final, MEM)
    fresh_end = fresh_flag[seg_count - 1]
    matrix_next = (
        fresh_end * memory_matrix[0].astype(jnp.float32)
        + contract_first(write_cols * end_rows[:, None], key_wide)
    ).astype(jnp.bfloat16)
    totals_next = fresh_end * key_totals[0] + jnp.dot(seen_final, key_sums, precision=highest)
    return (updated[None, None], matrix_next[None], totals_next[None])


def solution(mesh):
    return jax.shard_map(
        local,
        mesh=mesh,
        in_specs=(
            P("seg", "section", None, None),
            P("section", None, None),
            P("section", None, "seg"),
            P("section", None, "seg"),
            P("section", None),
            P("section", None),
            P("section", "seg", None),
            P("section", None),
            P("section", None),
        ),
        out_specs=(P("seg", "section", None, None), P("section", "seg", None), P("section", None)),
        check_vma=False,
    )
```

profile of v0, /device:TPU:1, one launch (start us, length us, event | category | flops | bytes accessed | tf_op | source)
XLA Modules:
  0.0 2270.6 jit_solution(1127673724252390452)
XLA Ops:
  10.1 51.4 %collective-permute-done = bf16[1,1,272,4096]{3,2,1,0:T(8,128)(2,1)S(1)} collective-permute-done((bf16[1,1,272,4096]{3,2,1,0:T(8,128)(2,1)}, bf16[1,1,272,4096]{3,2,1,0:T(8,128)(2,1)S(1)}, u32[]{:S(2)}, u32[]{:S(2)}) %collective-permute-start) | collective-permute-done | bytes 2228256 | tf_op jit(solution)/shard_map/ppermute | solution.py:13
  63.6 35.1 %all-gather.5.cloned.1.call-done = bf16[256,4096]{1,0:T(8,128)(2,1)} async-done(((bf16[16,4096]{1,0:T(8,128)(2,1)}), bf16[256,4096]{1,0:T(8,128)(2,1)}) %all-gather.5.cloned.1.call-update) | async-done | bytes 2097168 | tf_op jit(solution)/shard_map/all_gather | solution.py:67
  119.6 16.4 all-gather.7.cloned.1.call-done
  139.8 9.8 multiply_reduce_fusion.1
  154.0 75.3 %all-gather.9.cloned.1.call-done = bf16[1,4096,2048]{2,1,0:T(8,128)(2,1)} async-done(((bf16[1,256,2048]{2,1,0:T(8,128)(2,1)}), bf16[1,4096,2048]{2,1,0:T(8,128)(2,1)}) %all-gather.9.cloned.1.call-update) | async-done | bytes 16777232 | tf_op jit(solution)/shard_map/all_gather | solution.py:94
  229.4 9.0 fusion.4
  241.8 2007.7 %while.13 = (s32[]{:T(128)}, f32[256,4096]{1,0:T(8,128)}, f32[256,256]{1,0:T(8,128)}, f32[16,4096]{1,0:T(8,128)S(1)}, s32[]{:T(128)}, /*index=5*/s32[]{:T(128)}, s32[]{:T(128)}, s32[]{:T(128)}, u32[]{:T(128)}, u32[]{:T(128)}) while((s32[]{:T(128)}, f32[256,4096]{1,0:T(8,128)}, f32[256,256]{1,0:T(8,128)}, f32[16,4096]{1,0:T(8,128)S(1)}, ...), condition=%wide.region_6.7_spmd, body=%wide.region_4.6_spmd.sunk | while | flops 201654288 | bytes 5898477 | solution.py:111
  241.8 5.0 fusion.98
  246.8 118.6 %all-reduce.2.cloned.1.call-done = bf16[16,4096]{1,0:T(8,128)(2,1)} async-done(((bf16[16,4096]{1,0:T(8,128)(2,1)}), bf16[16,4096]{1,0:T(8,128)(2,1)}) %all-reduce.2.cloned.1.call-update) | async-done | bytes 131088 | tf_op jit(solution)/shard_map/while/body/eval_jaxpr/psum | solution.py:18
  367.1 5.0 fusion.98
  372.1 118.8 %all-reduce.2.cloned.1.call-done = bf16[16,4096]{1,0:T(8,128)(2,1)} async-done(((bf16[16,4096]{1,0:T(8,128)(2,1)}), bf16[16,4096]{1,0:T(8,128)(2,1)}) %all-reduce.2.cloned.1.call-update) | async-done | bytes 131088 | tf_op jit(solution)/shard_map/while/body/eval_jaxpr/psum | solution.py:18
  492.6 5.0 fusion.98
  497.6 118.8 %all-reduce.2.cloned.1.call-done = bf16[16,4096]{1,0:T(8,128)(2,1)} async-done(((bf16[16,4096]{1,0:T(8,128)(2,1)}), bf16[16,4096]{1,0:T(8,128)(2,1)}) %all-reduce.2.cloned.1.call-update) | async-done | bytes 131088 | tf_op jit(solution)/shard_map/while/body/eval_jaxpr/psum | solution.py:18
  618.0 5.0 fusion.98
  623.1 118.8 %all-reduce.2.cloned.1.call-done = bf16[16,4096]{1,0:T(8,128)(2,1)} async-done(((bf16[16,4096]{1,0:T(8,128)(2,1)}), bf16[16,4096]{1,0:T(8,128)(2,1)}) %all-reduce.2.cloned.1.call-update) | async-done | bytes 131088 | tf_op jit(solution)/shard_map/while/body/eval_jaxpr/psum | solution.py:18
  743.5 5.0 fusion.98
  748.6 118.8 %all-reduce.2.cloned.1.call-done = bf16[16,4096]{1,0:T(8,128)(2,1)} async-done(((bf16[16,4096]{1,0:T(8,128)(2,1)}), bf16[16,4096]{1,0:T(8,128)(2,1)}) %all-reduce.2.cloned.1.call-update) | async-done | bytes 131088 | tf_op jit(solution)/shard_map/while/body/eval_jaxpr/psum | solution.py:18
  869.0 5.0 fusion.98
  874.1 118.8 %all-reduce.2.cloned.1.call-done = bf16[16,4096]{1,0:T(8,128)(2,1)} async-done(((bf16[16,4096]{1,0:T(8,128)(2,1)}), bf16[16,4096]{1,0:T(8,128)(2,1)}) %all-reduce.2.cloned.1.call-update) | async-done | bytes 131088 | tf_op jit(solution)/shard_map/while/body/eval_jaxpr/psum | solution.py:18
  994.5 5.0 fusion.98
  999.6 118.8 %all-reduce.2.cloned.1.call-done = bf16[16,4096]{1,0:T(8,128)(2,1)} async-done(((bf16[16,4096]{1,0:T(8,128)(2,1)}), bf16[16,4096]{1,0:T(8,128)(2,1)}) %all-reduce.2.cloned.1.call-update) | async-done | bytes 131088 | tf_op jit(solution)/shard_map/while/body/eval_jaxpr/psum | solution.py:18
  1120.0 5.0 fusion.98
  1125.1 118.8 %all-reduce.2.cloned.1.call-done = bf16[16,4096]{1,0:T(8,128)(2,1)} async-done(((bf16[16,4096]{1,0:T(8,128)(2,1)}), bf16[16,4096]{1,0:T(8,128)(2,1)}) %all-reduce.2.cloned.1.call-update) | async-done | bytes 131088 | tf_op jit(solution)/shard_map/while/body/eval_jaxpr/psum | solution.py:18
  1250.6 118.8 %all-reduce.2.cloned.1.call-done = bf16[16,4096]{1,0:T(8,128)(2,1)} async-done(((bf16[16,4096]{1,0:T(8,128)(2,1)}), bf16[16,4096]{1,0:T(8,128)(2,1)}) %all-reduce.2.cloned.1.call-update) | async-done | bytes 131088 | tf_op jit(solution)/shard_map/while/body/eval_jaxpr/psum | solution.py:18
  1376.1 118.8 %all-reduce.2.cloned.1.call-done = bf16[16,4096]{1,0:T(8,128)(2,1)} async-done(((bf16[16,4096]{1,0:T(8,128)(2,1)}), bf16[16,4096]{1,0:T(8,128)(2,1)}) %all-reduce.2.cloned.1.call-update) | async-done | bytes 131088 | tf_op jit(solution)/shard_map/while/body/eval_jaxpr/psum | solution.py:18
  1501.6 118.8 %all-reduce.2.cloned.1.call-done = bf16[16,4096]{1,0:T(8,128)(2,1)} async-done(((bf16[16,4096]{1,0:T(8,128)(2,1)}), bf16[16,4096]{1,0:T(8,128)(2,1)}) %all-reduce.2.cloned.1.call-update) | async-done | bytes 131088 | tf_op jit(solution)/shard_map/while/body/eval_jaxpr/psum | solution.py:18
  1627.0 118.8 %all-reduce.2.cloned.1.call-done = bf16[16,4096]{1,0:T(8,128)(2,1)} async-done(((bf16[16,4096]{1,0:T(8,128)(2,1)}), bf16[16,4096]{1,0:T(8,128)(2,1)}) %all-reduce.2.cloned.1.call-update) | async-done | bytes 131088 | tf_op jit(solution)/shard_map/while/body/eval_jaxpr/psum | solution.py:18
  1752.5 118.8 %all-reduce.2.cloned.1.call-done = bf16[16,4096]{1,0:T(8,128)(2,1)} async-done(((bf16[16,4096]{1,0:T(8,128)(2,1)}), bf16[16,4096]{1,0:T(8,128)(2,1)}) %all-reduce.2.cloned.1.call-update) | async-done | bytes 131088 | tf_op jit(solution)/shard_map/while/body/eval_jaxpr/psum | solution.py:18
  1878.0 118.8 %all-reduce.2.cloned.1.call-done = bf16[16,4096]{1,0:T(8,128)(2,1)} async-done(((bf16[16,4096]{1,0:T(8,128)(2,1)}), bf16[16,4096]{1,0:T(8,128)(2,1)}) %all-reduce.2.cloned.1.call-update) | async-done | bytes 131088 | tf_op jit(solution)/shard_map/while/body/eval_jaxpr/psum | solution.py:18
  2003.5 118.8 %all-reduce.2.cloned.1.call-done = bf16[16,4096]{1,0:T(8,128)(2,1)} async-done(((bf16[16,4096]{1,0:T(8,128)(2,1)}), bf16[16,4096]{1,0:T(8,128)(2,1)}) %all-reduce.2.cloned.1.call-update) | async-done | bytes 131088 | tf_op jit(solution)/shard_map/while/body/eval_jaxpr/psum | solution.py:18
  2129.1 118.8 %all-reduce.2.cloned.1.call-done = bf16[16,4096]{1,0:T(8,128)(2,1)} async-done(((bf16[16,4096]{1,0:T(8,128)(2,1)}), bf16[16,4096]{1,0:T(8,128)(2,1)}) %all-reduce.2.cloned.1.call-update) | async-done | bytes 131088 | tf_op jit(solution)/shard_map/while/body/eval_jaxpr/psum | solution.py:18
  2253.7 10.3 fusion.11
  (136 shorter events, 108.3 us)
Async XLA Ops:
  7.2 98.1 %copy-start = (bf16[1,4096,256]{2,1,0:T(8,128)(2,1)S(1)}, bf16[1,4096,256]{2,1,0:T(8,128)(2,1)}, u32[]{:S(2)}) copy-start(bf16[1,4096,256]{2,1,0:T(8,128)(2,1)} %param.14) | copy-start | bytes 6291460
  7.2 91.5 %all-gather.5.cloned.1.call-start = ((), (), s32[]{:S(2)}) async-start(), calls=%async_computation.1 | async-start | bytes 2228224 | tf_op jit(solution)/shard_map/all_gather | solution.py:67
  7.2 54.2 %collective-permute-start = (bf16[1,1,272,4096]{3,2,1,0:T(8,128)(2,1)}, bf16[1,1,272,4096]{3,2,1,0:T(8,128)(2,1)S(1)}, u32[]{:S(2)}, u32[]{:S(2)}) collective-permute-start(bf16[1,1,272,4096]{3,2,1,0:T(8,128)(2,1)} %param.11), channel_id=1, source_target_pairs={{0,1},{1,2},{2,3},{3,4},{4,5},{5,6},{6,7},{7,0},{8,9},{9,10},{10,1... | collective-permute-start | bytes 6684680 | tf_op jit(solution)/shard_map/ppermute | solution.py:13
  62.0 36.7 %copy-start.6 = (bf16[1,4096,128]{2,1,0:T(8,128)(2,1)S(1)}, bf16[1,4096,128]{2,1,0:T(8,128)(2,1)}, u32[]{:S(2)}) copy-start(bf16[1,4096,128]{2,1,0:T(8,128)(2,1)} %param.13) | copy-start | bytes 3145732
  63.6 38.8 %copy-start.12 = (s32[1,16]{1,0:T(1,128)S(1)}, s32[1,16]{1,0:T(1,128)}, u32[]{:S(2)}) copy-start(s32[1,16]{1,0:T(1,128)} %param.19) | copy-start | bytes 196
  63.6 72.5 %all-gather.7.cloned.1.call-start = ((), (), s32[]{:S(2)}) async-start(), calls=%async_computation.2 | async-start | bytes 1114112 | tf_op jit(solution)/shard_map/all_gather | solution.py:73
  101.6 127.7 %all-gather.9.cloned.1.call-start = ((), (), s32[]{:S(2)}) async-start(), calls=%async_computation.3 | async-start | bytes 17825792 | tf_op jit(solution)/shard_map/all_gather | solution.py:94
  105.3 7.5 copy-start.10
  108.2 29.6 %copy-start.9 = (f32[1,2048]{1,0:T(1,128)S(1)}, f32[1,2048]{1,0:T(1,128)}, u32[]{:S(2)}) copy-start(f32[1,2048]{1,0:T(1,128)} %param.18) | copy-start | bytes 24580
  108.2 10.6 all-to-all-start
  136.0 3.7 copy-start.3
  139.8 11.8 copy-start.1
  229.4 9.0 copy-start.7
  238.3 3.4 copy-start.11
  241.8 123.7 %all-reduce.2.cloned.1.call-start = ((), (), s32[]{:S(2)}) async-start(), calls=%async_computation.4 | async-start | bytes 262144 | tf_op jit(solution)/shard_map/while/body/eval_jaxpr/psum | solution.py:18
  367.1 123.9 %all-reduce.2.cloned.1.call-start = ((), (), s32[]{:S(2)}) async-start(), calls=%async_computation.4 | async-start | bytes 262144 | tf_op jit(solution)/shard_map/while/body/eval_jaxpr/psum | solution.py:18
  492.5 123.9 %all-reduce.2.cloned.1.call-start = ((), (), s32[]{:S(2)}) async-start(), calls=%async_computation.4 | async-start | bytes 262144 | tf_op jit(solution)/shard_map/while/body/eval_jaxpr/psum | solution.py:18
  618.0 123.9 %all-reduce.2.cloned.1.call-start = ((), (), s32[]{:S(2)}) async-start(), calls=%async_computation.4 | async-start | bytes 262144 | tf_op jit(solution)/shard_map/while/body/eval_jaxpr/psum | solution.py:18
  743.5 123.9 %all-reduce.2.cloned.1.call-start = ((), (), s32[]{:S(2)}) async-start(), calls=%async_computation.4 | async-start | bytes 262144 | tf_op jit(solution)/shard_map/while/body/eval_jaxpr/psum | solution.py:18
  869.0 123.9 %all-reduce.2.cloned.1.call-start = ((), (), s32[]{:S(2)}) async-start(), calls=%async_computation.4 | async-start | bytes 262144 | tf_op jit(solution)/shard_map/while/body/eval_jaxpr/psum | solution.py:18
  994.5 123.9 %all-reduce.2.cloned.1.call-start = ((), (), s32[]{:S(2)}) async-start(), calls=%async_computation.4 | async-start | bytes 262144 | tf_op jit(solution)/shard_map/while/body/eval_jaxpr/psum | solution.py:18
  1120.0 123.9 %all-reduce.2.cloned.1.call-start = ((), (), s32[]{:S(2)}) async-start(), calls=%async_computation.4 | async-start | bytes 262144 | tf_op jit(solution)/shard_map/while/body/eval_jaxpr/psum | solution.py:18
  1245.5 123.9 %all-reduce.2.cloned.1.call-start = ((), (), s32[]{:S(2)}) async-start(), calls=%async_computation.4 | async-start | bytes 262144 | tf_op jit(solution)/shard_map/while/body/eval_jaxpr/psum | solution.py:18
  1371.0 123.9 %all-reduce.2.cloned.1.call-start = ((), (), s32[]{:S(2)}) async-start(), calls=%async_computation.4 | async-start | bytes 262144 | tf_op jit(solution)/shard_map/while/body/eval_jaxpr/psum | solution.py:18
  1496.5 123.9 %all-reduce.2.cloned.1.call-start = ((), (), s32[]{:S(2)}) async-start(), calls=%async_computation.4 | async-start | bytes 262144 | tf_op jit(solution)/shard_map/while/body/eval_jaxpr/psum | solution.py:18
  1622.0 123.9 %all-reduce.2.cloned.1.call-start = ((), (), s32[]{:S(2)}) async-start(), calls=%async_computation.4 | async-start | bytes 262144 | tf_op jit(solution)/shard_map/while/body/eval_jaxpr/psum | solution.py:18
  1747.5 123.9 %all-reduce.2.cloned.1.call-start = ((), (), s32[]{:S(2)}) async-start(), calls=%async_computation.4 | async-start | bytes 262144 | tf_op jit(solution)/shard_map/while/body/eval_jaxpr/psum | solution.py:18
  1873.0 123.9 %all-reduce.2.cloned.1.call-start = ((), (), s32[]{:S(2)}) async-start(), calls=%async_computation.4 | async-start | bytes 262144 | tf_op jit(solution)/shard_map/while/body/eval_jaxpr/psum | solution.py:18
  1998.5 123.9 %all-reduce.2.cloned.1.call-start = ((), (), s32[]{:S(2)}) async-start(), calls=%async_computation.4 | async-start | bytes 262144 | tf_op jit(solution)/shard_map/while/body/eval_jaxpr/psum | solution.py:18
  2124.0 123.9 %all-reduce.2.cloned.1.call-start = ((), (), s32[]{:S(2)}) async-start(), calls=%async_computation.4 | async-start | bytes 262144 | tf_op jit(solution)/shard_map/while/body/eval_jaxpr/psum | solution.py:18
  2249.5 4.2 copy-start.4
  2249.5 4.2 copy-start.8
  (2 other events, 3.4 us)
Sparse Core Ops, SparseCore 0:
  63.7 34.9 all-gather.4
  101.8 34.2 all-gather.6
  137.8 91.5 all-gather.8
  247.0 118.4 all-reduce.1
  372.2 118.6 all-reduce.1
  497.7 118.6 all-reduce.1
  623.2 118.6 all-reduce.1
  748.7 118.6 all-reduce.1
  874.2 118.6 all-reduce.1
  999.7 118.6 all-reduce.1
  1125.2 118.6 all-reduce.1
  1250.7 118.6 all-reduce.1
  1376.2 118.6 all-reduce.1
  1501.7 118.6 all-reduce.1
  1627.2 118.6 all-reduce.1
  1752.7 118.6 all-reduce.1
  1878.1 118.6 all-reduce.1
  2003.7 118.6 all-reduce.1
  2129.2 118.6 all-reduce.1
where the time goes:
time: 2270 us
  waiting for transfers between devices  2080 us (92%)
  matrix products  126 us (6%)
  other arithmetic  34.7 us (2%)
    psum x16, waiting for transfers between devices, from_root(): return lax.psum(block, axis)  1900 us
    dot_general x17, matrix products, contract_first(): lax.dot_general(left_rows, right_rows, (((0,), (0,)), ((), ())), precisio...  84.8 us
    all_gather x1, waiting for transfers between devices, local(): lax.all_gather(memory_matrix[0], 'seg', axis=0, tiled=True)  75.3 us
    ppermute x1, waiting for transfers between devices, shifted(): lax.ppermute(shard, axis, [(i, (i + by) % size) for i in range(size)])  51.4 us
  transfers between devices with their start and end apart: 21, of which 21 were waited for; matrix products, arithmetic and copies ran while one was open for 1% of the time, Pallas kernels for 0%

commit v1 on v0

--- a/solution.py
+++ b/solution.py
@@ -6,6 +6,11 @@
 MEM = 16
 highest = lax.Precision.HIGHEST
 epsilon = 1e-05
+
+
+def supply_all_inputs(local_x, dev_axis, pos_dim):
+    mid_arr = lax.all_to_all(jnp.stack([local_x] * lax.axis_size(dev_axis)), dev_axis, 0, 0)
+    return jnp.concatenate(mid_arr, axis=pos_dim)
 
 
 def shifted(shard, axis, by):
@@ -91,7 +96,7 @@
     mixing = seen_cols * key_gram * (gate_rates / key_scales)[None, :]
     my_keys = lax.dynamic_slice_in_dim(key_rows, my_index * MEM, MEM, 0)
     probes = jnp.concatenate([queries, my_keys], axis=0)
-    probed_all = contract_last(probes, lax.all_gather(memory_matrix[0], "seg", axis=0, tiled=True))
+    probed_all = contract_last(probes, supply_all_inputs(memory_matrix[0], "seg", 0))
     base_read = probed_all[:row_count]
     probed_keys = probed_all[row_count:]
     my_fresh = fresh_flag[my_index]

time: 2270 us -> 2380 us (1.048)
  waiting for transfers between devices: 2080 us -> 2160 us
    all_gather x1, waiting for transfers between devices: 16.4 us -> 161 us  [local(): key_rows = lax.all_gather(key_part, 'seg', axis=1, tiled=True)]
    all_gather x1 -> x0, waiting for transfers between devices: 75.3 us -> none  [local(): lax.all_gather(memory_matrix[0], 'seg', axis=0, tiled=True)]
  transfers between devices with their start and end apart: 21 -> 20, of which waited for: 21 -> 19; matrix products, arithmetic and copies ran while one was open for 1% -> 1% of each run, Pallas kernels for 0% -> 0%
where the time goes in v1:
time: 2380 us; the launch traced here: 2370 us
  waiting for transfers between devices  2160 us (91%)
  matrix products  125 us (5%)
  other arithmetic  35.1 us (1%)
    psum x16, waiting for transfers between devices, from_root(): return lax.psum(block, axis)  1910 us
    all_gather x1, waiting for transfers between devices, local(): key_rows = lax.all_gather(key_part, 'seg', axis=1, tiled=True)  161 us
    dot_general x17, matrix products, contract_first(): lax.dot_general(left_rows, right_rows, (((0,), (0,)), ((), ())), precisio...  83.3 us
    ppermute x1, waiting for transfers between devices, shifted(): lax.ppermute(shard, axis, [(i, (i + by) % size) for i in range(size)])  51.4 us
  transfers between devices with their start and end apart: 20, of which 19 were waited for; matrix products, arithmetic and copies ran while one was open for 1% of the time, Pallas kernels for 0%

profile of v1, /device:TPU:1, one launch (start us, length us, event | category | flops | bytes accessed | tf_op | source)
XLA Modules:
  0.0 2374.4 jit_solution(1279155473250602112)
XLA Ops:
  10.1 51.4 %collective-permute-done = bf16[1,1,272,4096]{3,2,1,0:T(8,128)(2,1)S(1)} collective-permute-done((bf16[1,1,272,4096]{3,2,1,0:T(8,128)(2,1)}, bf16[1,1,272,4096]{3,2,1,0:T(8,128)(2,1)S(1)}, u32[]{:S(2)}, u32[]{:S(2)}) %collective-permute-start) | collective-permute-done | bytes 2228256 | tf_op jit(solution)/shard_map/ppermute | solution.py:18
  64.1 35.1 %all-gather.3.cloned.1.call-done = bf16[256,4096]{1,0:T(8,128)(2,1)} async-done(((bf16[16,4096]{1,0:T(8,128)(2,1)}), bf16[256,4096]{1,0:T(8,128)(2,1)}) %all-gather.3.cloned.1.call-update) | async-done | bytes 2097168 | tf_op jit(solution)/shard_map/all_gather | solution.py:72
  101.6 10.3 all_to_all.14
  111.9 5.9 stack.3
  117.8 5.7 all-to-all-start
  138.8 161.1 %all-gather.5.cloned.1.call-done = bf16[256,2048]{1,0:T(8,128)(2,1)} async-done(((bf16[256,128]{1,0:T(8,128)(2,1)}), bf16[256,2048]{1,0:T(8,128)(2,1)}) %all-gather.5.cloned.1.call-update) | async-done | bytes 1048592 | tf_op jit(solution)/shard_map/all_gather | solution.py:78
  304.2 12.3 multiply_reduce_fusion.1
  320.2 9.1 fusion.36
  332.8 2020.7 %while.13 = (s32[]{:T(128)}, f32[256,4096]{1,0:T(8,128)}, f32[256,256]{1,0:T(8,128)S(1)}, f32[16,4096]{1,0:T(8,128)S(1)}, s32[]{:T(128)}, /*index=5*/s32[]{:T(128)}, s32[]{:T(128)}, s32[]{:T(128)}, u32[]{:T(128)}, u32[]{:T(128)}) while((s32[]{:T(128)}, f32[256,4096]{1,0:T(8,128)}, f32[256,256]{1,0:T(8,128)S(1)}, f32[16,4096]{1,0:T(8,128)S(1)}, ...), condition=%wide.region_6.7_spmd, body=%wide.region_4.6_spmd.sunk | while | flops 201654288 | bytes 5898477 | solution.py:116
  337.8 132.8 %all-reduce.2.cloned.1.call-done = bf16[16,4096]{1,0:T(8,128)(2,1)} async-done(((bf16[16,4096]{1,0:T(8,128)(2,1)}), bf16[16,4096]{1,0:T(8,128)(2,1)}) %all-reduce.2.cloned.1.call-update) | async-done | bytes 131088 | tf_op jit(solution)/shard_map/while/body/eval_jaxpr/psum | solution.py:23
  477.1 118.8 %all-reduce.2.cloned.1.call-done = bf16[16,4096]{1,0:T(8,128)(2,1)} async-done(((bf16[16,4096]{1,0:T(8,128)(2,1)}), bf16[16,4096]{1,0:T(8,128)(2,1)}) %all-reduce.2.cloned.1.call-update) | async-done | bytes 131088 | tf_op jit(solution)/shard_map/while/body/eval_jaxpr/psum | solution.py:23
  602.6 118.8 %all-reduce.2.cloned.1.call-done = bf16[16,4096]{1,0:T(8,128)(2,1)} async-done(((bf16[16,4096]{1,0:T(8,128)(2,1)}), bf16[16,4096]{1,0:T(8,128)(2,1)}) %all-reduce.2.cloned.1.call-update) | async-done | bytes 131088 | tf_op jit(solution)/shard_map/while/body/eval_jaxpr/psum | solution.py:23
  728.0 118.8 %all-reduce.2.cloned.1.call-done = bf16[16,4096]{1,0:T(8,128)(2,1)} async-done(((bf16[16,4096]{1,0:T(8,128)(2,1)}), bf16[16,4096]{1,0:T(8,128)(2,1)}) %all-reduce.2.cloned.1.call-update) | async-done | bytes 131088 | tf_op jit(solution)/shard_map/while/body/eval_jaxpr/psum | solution.py:23
  853.4 118.8 %all-reduce.2.cloned.1.call-done = bf16[16,4096]{1,0:T(8,128)(2,1)} async-done(((bf16[16,4096]{1,0:T(8,128)(2,1)}), bf16[16,4096]{1,0:T(8,128)(2,1)}) %all-reduce.2.cloned.1.call-update) | async-done | bytes 131088 | tf_op jit(solution)/shard_map/while/body/eval_jaxpr/psum | solution.py:23
  978.8 118.8 %all-reduce.2.cloned.1.call-done = bf16[16,4096]{1,0:T(8,128)(2,1)} async-done(((bf16[16,4096]{1,0:T(8,128)(2,1)}), bf16[16,4096]{1,0:T(8,128)(2,1)}) %all-reduce.2.cloned.1.call-update) | async-done | bytes 131088 | tf_op jit(solution)/shard_map/while/body/eval_jaxpr/psum | solution.py:23
  1104.3 118.8 %all-reduce.2.cloned.1.call-done = bf16[16,4096]{1,0:T(8,128)(2,1)} async-done(((bf16[16,4096]{1,0:T(8,128)(2,1)}), bf16[16,4096]{1,0:T(8,128)(2,1)}) %all-reduce.2.cloned.1.call-update) | async-done | bytes 131088 | tf_op jit(solution)/shard_map/while/body/eval_jaxpr/psum | solution.py:23
  1229.7 118.8 %all-reduce.2.cloned.1.call-done = bf16[16,4096]{1,0:T(8,128)(2,1)} async-done(((bf16[16,4096]{1,0:T(8,128)(2,1)}), bf16[16,4096]{1,0:T(8,128)(2,1)}) %all-reduce.2.cloned.1.call-update) | async-done | bytes 131088 | tf_op jit(solution)/shard_map/while/body/eval_jaxpr/psum | solution.py:23
  1350.1 5.0 fusion.98
  1355.1 118.8 %all-reduce.2.cloned.1.call-done = bf16[16,4096]{1,0:T(8,128)(2,1)} async-done(((bf16[16,4096]{1,0:T(8,128)(2,1)}), bf16[16,4096]{1,0:T(8,128)(2,1)}) %all-reduce.2.cloned.1.call-update) | async-done | bytes 131088 | tf_op jit(solution)/shard_map/while/body/eval_jaxpr/psum | solution.py:23
  1475.6 5.0 fusion.98
  1480.5 118.8 %all-reduce.2.cloned.1.call-done = bf16[16,4096]{1,0:T(8,128)(2,1)} async-done(((bf16[16,4096]{1,0:T(8,128)(2,1)}), bf16[16,4096]{1,0:T(8,128)(2,1)}) %all-reduce.2.cloned.1.call-update) | async-done | bytes 131088 | tf_op jit(solution)/shard_map/while/body/eval_jaxpr/psum | solution.py:23
  1601.0 5.0 fusion.98
  1606.0 118.8 %all-reduce.2.cloned.1.call-done = bf16[16,4096]{1,0:T(8,128)(2,1)} async-done(((bf16[16,4096]{1,0:T(8,128)(2,1)}), bf16[16,4096]{1,0:T(8,128)(2,1)}) %all-reduce.2.cloned.1.call-update) | async-done | bytes 131088 | tf_op jit(solution)/shard_map/while/body/eval_jaxpr/psum | solution.py:23
  1726.4 5.0 fusion.98
  1731.4 118.8 %all-reduce.2.cloned.1.call-done = bf16[16,4096]{1,0:T(8,128)(2,1)} async-done(((bf16[16,4096]{1,0:T(8,128)(2,1)}), bf16[16,4096]{1,0:T(8,128)(2,1)}) %all-reduce.2.cloned.1.call-update) | async-done | bytes 131088 | tf_op jit(solution)/shard_map/while/body/eval_jaxpr/psum | solution.py:23
  1851.8 5.0 fusion.98
  1856.8 118.8 %all-reduce.2.cloned.1.call-done = bf16[16,4096]{1,0:T(8,128)(2,1)} async-done(((bf16[16,4096]{1,0:T(8,128)(2,1)}), bf16[16,4096]{1,0:T(8,128)(2,1)}) %all-reduce.2.cloned.1.call-update) | async-done | bytes 131088 | tf_op jit(solution)/shard_map/while/body/eval_jaxpr/psum | solution.py:23
  1977.2 5.0 fusion.98
  1982.2 118.8 %all-reduce.2.cloned.1.call-done = bf16[16,4096]{1,0:T(8,128)(2,1)} async-done(((bf16[16,4096]{1,0:T(8,128)(2,1)}), bf16[16,4096]{1,0:T(8,128)(2,1)}) %all-reduce.2.cloned.1.call-update) | async-done | bytes 131088 | tf_op jit(solution)/shard_map/while/body/eval_jaxpr/psum | solution.py:23
  2107.6 118.8 %all-reduce.2.cloned.1.call-done = bf16[16,4096]{1,0:T(8,128)(2,1)} async-done(((bf16[16,4096]{1,0:T(8,128)(2,1)}), bf16[16,4096]{1,0:T(8,128)(2,1)}) %all-reduce.2.cloned.1.call-update) | async-done | bytes 131088 | tf_op jit(solution)/shard_map/while/body/eval_jaxpr/psum | solution.py:23
  2233.1 118.8 %all-reduce.2.cloned.1.call-done = bf16[16,4096]{1,0:T(8,128)(2,1)} async-done(((bf16[16,4096]{1,0:T(8,128)(2,1)}), bf16[16,4096]{1,0:T(8,128)(2,1)}) %all-reduce.2.cloned.1.call-update) | async-done | bytes 131088 | tf_op jit(solution)/shard_map/while/body/eval_jaxpr/psum | solution.py:23
  2357.4 10.1 fusion.9
  (149 shorter events, 114.3 us)
Async XLA Ops:
  7.2 92.0 %copy-start = (bf16[1,4096,256]{2,1,0:T(8,128)(2,1)S(1)}, bf16[1,4096,256]{2,1,0:T(8,128)(2,1)}, u32[]{:S(2)}) copy-start(bf16[1,4096,256]{2,1,0:T(8,128)(2,1)} %param.14) | copy-start | bytes 6291460
  7.2 92.0 %all-gather.3.cloned.1.call-start = ((), (), s32[]{:S(2)}) async-start(), calls=%async_computation.2 | async-start | bytes 2228224 | tf_op jit(solution)/shard_map/all_gather | solution.py:72
  7.2 54.2 %collective-permute-start = (bf16[1,1,272,4096]{3,2,1,0:T(8,128)(2,1)}, bf16[1,1,272,4096]{3,2,1,0:T(8,128)(2,1)S(1)}, u32[]{:S(2)}, u32[]{:S(2)}) collective-permute-start(bf16[1,1,272,4096]{3,2,1,0:T(8,128)(2,1)} %param.11), channel_id=1, source_target_pairs={{0,1},{1,2},{2,3},{3,4},{4,5},{5,6},{6,7},{7,0},{8,9},{9,10},{10,1... | collective-permute-start | bytes 6684680 | tf_op jit(solution)/shard_map/ppermute | solution.py:18
  99.2 12.7 copy-start.6
  117.8 5.7 copy-start.5
  117.8 202.3 %all-to-all-start = ((bf16[16,256,2048]{2,1,0:T(8,128)(2,1)}), bf16[16,256,2048]{2,1,0:T(8,128)(2,1)}, u32[]{:S(2)}, u32[]{:S(2)}) async-start(bf16[16,256,2048]{2,1,0:T(8,128)(2,1)} %stack.3), calls=%async_computation | async-start | bytes 33554432 | tf_op jit(solution)/shard_map/all_to_all | solution.py:12
  123.5 176.4 %all-gather.5.cloned.1.call-start = ((), (), s32[]{:S(2)}) async-start(), calls=%async_computation.3 | async-start | bytes 1114112 | tf_op jit(solution)/shard_map/all_gather | solution.py:78
  138.7 165.2 %copy-start.16 = (f32[1,256]{1,0:T(1,128)S(1)}, f32[1,256]{1,0:T(1,128)}, u32[]{:S(2)}) copy-start(f32[1,256]{1,0:T(1,128)} %fusion.63) | copy-start | bytes 3076
  138.7 165.4 %copy-start.18 = (f32[272]{0:T(512)S(1)}, f32[272]{0:T(512)}, u32[]{:S(2)}) copy-start(f32[272]{0:T(512)} %copy-done.17) | copy-start | bytes 3268
  304.1 13.1 copy-start.9
  304.1 14.3 copy-start.2
  304.1 14.3 copy-start.15
  332.8 2020.8 %copy-start.14 = (f32[256]{0:T(256)S(1)}, f32[256]{0:T(256)}, u32[]{:S(2)}) copy-start(f32[256]{0:T(256)} %mul.175) | copy-start | bytes 3076
  332.8 137.8 %all-reduce.2.cloned.1.call-start = ((), (), s32[]{:S(2)}) async-start(), calls=%async_computation.4 | async-start | bytes 262144 | tf_op jit(solution)/shard_map/while/body/eval_jaxpr/psum | solution.py:23
  472.2 123.8 %all-reduce.2.cloned.1.call-start = ((), (), s32[]{:S(2)}) async-start(), calls=%async_computation.4 | async-start | bytes 262144 | tf_op jit(solution)/shard_map/while/body/eval_jaxpr/psum | solution.py:23
  597.6 123.8 %all-reduce.2.cloned.1.call-start = ((), (), s32[]{:S(2)}) async-start(), calls=%async_computation.4 | async-start | bytes 262144 | tf_op jit(solution)/shard_map/while/body/eval_jaxpr/psum | solution.py:23
  723.0 123.8 %all-reduce.2.cloned.1.call-start = ((), (), s32[]{:S(2)}) async-start(), calls=%async_computation.4 | async-start | bytes 262144 | tf_op jit(solution)/shard_map/while/body/eval_jaxpr/psum | solution.py:23
  848.4 123.8 %all-reduce.2.cloned.1.call-start = ((), (), s32[]{:S(2)}) async-start(), calls=%async_computation.4 | async-start | bytes 262144 | tf_op jit(solution)/shard_map/while/body/eval_jaxpr/psum | solution.py:23
  973.9 123.8 %all-reduce.2.cloned.1.call-start = ((), (), s32[]{:S(2)}) async-start(), calls=%async_computation.4 | async-start | bytes 262144 | tf_op jit(solution)/shard_map/while/body/eval_jaxpr/psum | solution.py:23
  1099.3 123.8 %all-reduce.2.cloned.1.call-start = ((), (), s32[]{:S(2)}) async-start(), calls=%async_computation.4 | async-start | bytes 262144 | tf_op jit(solution)/shard_map/while/body/eval_jaxpr/psum | solution.py:23
  1224.7 123.8 %all-reduce.2.cloned.1.call-start = ((), (), s32[]{:S(2)}) async-start(), calls=%async_computation.4 | async-start | bytes 262144 | tf_op jit(solution)/shard_map/while/body/eval_jaxpr/psum | solution.py:23
  1350.1 123.8 %all-reduce.2.cloned.1.call-start = ((), (), s32[]{:S(2)}) async-start(), calls=%async_computation.4 | async-start | bytes 262144 | tf_op jit(solution)/shard_map/while/body/eval_jaxpr/psum | solution.py:23
  1475.6 123.8 %all-reduce.2.cloned.1.call-start = ((), (), s32[]{:S(2)}) async-start(), calls=%async_computation.4 | async-start | bytes 262144 | tf_op jit(solution)/shard_map/while/body/eval_jaxpr/psum | solution.py:23
  1601.0 123.8 %all-reduce.2.cloned.1.call-start = ((), (), s32[]{:S(2)}) async-start(), calls=%async_computation.4 | async-start | bytes 262144 | tf_op jit(solution)/shard_map/while/body/eval_jaxpr/psum | solution.py:23
  1726.4 123.8 %all-reduce.2.cloned.1.call-start = ((), (), s32[]{:S(2)}) async-start(), calls=%async_computation.4 | async-start | bytes 262144 | tf_op jit(solution)/shard_map/while/body/eval_jaxpr/psum | solution.py:23
  1851.8 123.8 %all-reduce.2.cloned.1.call-start = ((), (), s32[]{:S(2)}) async-start(), calls=%async_computation.4 | async-start | bytes 262144 | tf_op jit(solution)/shard_map/while/body/eval_jaxpr/psum | solution.py:23
  1977.2 123.8 %all-reduce.2.cloned.1.call-start = ((), (), s32[]{:S(2)}) async-start(), calls=%async_computation.4 | async-start | bytes 262144 | tf_op jit(solution)/shard_map/while/body/eval_jaxpr/psum | solution.py:23
  2102.6 123.8 %all-reduce.2.cloned.1.call-start = ((), (), s32[]{:S(2)}) async-start(), calls=%async_computation.4 | async-start | bytes 262144 | tf_op jit(solution)/shard_map/while/body/eval_jaxpr/psum | solution.py:23
  2228.1 123.8 %all-reduce.2.cloned.1.call-start = ((), (), s32[]{:S(2)}) async-start(), calls=%async_computation.4 | async-start | bytes 262144 | tf_op jit(solution)/shard_map/while/body/eval_jaxpr/psum | solution.py:23
  2353.5 3.9 copy-start.4
  2353.5 3.9 copy-start.8
  2357.4 10.2 copy-start.1
  (8 other events, 13.7 us)
Sparse Core Ops, SparseCore 0:
  64.2 34.9 all-gather.2
  126.3 173.5 all-gather.4
  337.9 132.5 all-reduce.1
  477.3 118.6 all-reduce.1
  602.7 118.6 all-reduce.1
  728.1 118.6 all-reduce.1
  853.5 118.6 all-reduce.1
  979.0 118.6 all-reduce.1
  1104.4 118.6 all-reduce.1
  1229.8 118.6 all-reduce.1
  1355.2 118.6 all-reduce.1
  1480.7 118.6 all-reduce.1
  1606.1 118.6 all-reduce.1
  1731.5 118.6 all-reduce.1
  1856.9 118.6 all-reduce.1
  1982.3 118.6 all-reduce.1
  2107.8 118.6 all-reduce.1
  2233.2 118.6 all-reduce.1
